TPU v7x, 32 devices: a whole 2x2x4 slice. The times are simulated.
32 devices in a mesh: fsdp: 8 (over z, y), ctx: 2 (over x), tensor: 2 (over core).
Axes of the slice: x: 2, y: 2, z: 4, core: 2. Of those that a mesh axis runs over, the one named last changes fastest.
Arguments:
- block_input: bfloat16 [8, 1024, 1024], P('fsdp', 'ctx'), may hold values from -6 to 6
- operator_gain: bfloat16 [1024], P('fsdp'), may hold values from 0.5 to 1.5
- query_weight: bfloat16 [1024, 1024], P('fsdp', 'tensor'), may hold values from -0.1875 to 0.1875
- key_weight: bfloat16 [1024, 512], P('fsdp', 'tensor'), may hold values from -0.1875 to 0.1875
- value_weight: bfloat16 [1024, 512], P('fsdp', 'tensor'), may hold values from -0.1875 to 0.1875
- output_weight: bfloat16 [1024, 1024], P('tensor', 'fsdp'), may hold values from -0.75 to 0.75
- feedforward_gain: bfloat16 [1024], P('fsdp'), may hold values from 0.5 to 1.5
- gate_weight: bfloat16 [1024, 4608], P('fsdp', 'tensor'), may hold values from -0.1875 to 0.1875
- up_weight: bfloat16 [1024, 4608], P('fsdp', 'tensor'), may hold values from -0.1875 to 0.1875
- down_weight: bfloat16 [4608, 1024], P('tensor', 'fsdp'), may hold values from -0.09375 to 0.09375
- query_gain: bfloat16 [64], P('fsdp'), may hold values from 0.6 to 4
- key_gain: bfloat16 [64], P('fsdp'), may hold values from 0.6 to 4
- cotangent: bfloat16 [8, 1024, 1024], P('fsdp', 'ctx'), may hold values from -6 to 6
Outputs:
- block_output: bfloat16 [8, 1024, 1024], P('fsdp', 'ctx')
- input_grad: float32 [8, 1024, 1024], P('fsdp', 'ctx')
- operator_gain_grad: float32 [1024], P('fsdp')
- query_weight_grad: float32 [1024, 1024], P('fsdp', 'tensor')
- key_weight_grad: float32 [1024, 512], P('fsdp', 'tensor')
- value_weight_grad: float32 [1024, 512], P('fsdp', 'tensor')
- output_weight_grad: float32 [1024, 1024], P('tensor', 'fsdp')
- feedforward_gain_grad: float32 [1024], P('fsdp')
- gate_weight_grad: float32 [1024, 4608], P('fsdp', 'tensor')
- up_weight_grad: float32 [1024, 4608], P('fsdp', 'tensor')
- down_weight_grad: float32 [4608, 1024], P('tensor', 'fsdp')
- query_gain_grad: float32 [64], P('fsdp')
- key_gain_grad: float32 [64], P('fsdp')
All inputs are finite; a program needn't handle non-finite values.
Results may differ from a plain program's by a relative error of at most 0.024.
The roundings to bfloat16 on the way count: a program that leaves them out, or rounds other values in their place, can miss the bound.
Values may be sent and summed in bfloat16 or wider, within the bound.
A program may use at most 192 MiB of HBM per device.

v0:
```python
import jax
import jax.numpy as jnp
from jax import lax
from jax.sharding import PartitionSpec as P

EPS = 1e-05
THETA = 1000000.0


def as_sent(array):
    return jax.tree.map(lambda a: a.astype(jnp.bfloat16) if a.dtype == jnp.float32 else a, array)


def rms_scale(values_in, gain):
    return (
        values_in * lax.rsqrt(jnp.mean(values_in * values_in, axis=-1, keepdims=True) + EPS) * gain
    )


def rotary_tables(positions, head_width):
    half_width = head_width // 2
    freqs = THETA ** (-jnp.arange(half_width).astype(jnp.float32) * 2.0 / head_width)
    angles = positions.astype(jnp.float32)[:, None] * freqs[None, :]
    return (jnp.cos(angles), jnp.sin(angles))


def rotate_halves(heads_in, cosine, sine):
    half_width = heads_in.shape[-1] // 2
    front_half = heads_in[..., :half_width]
    back_half = heads_in[..., half_width:]
    cos_rows = cosine[:, None, :]
    sin_rows = sine[:, None, :]
    return jnp.concatenate(
        [
            front_half * cos_rows - back_half * sin_rows,
            back_half * cos_rows + front_half * sin_rows,
        ],
        axis=-1,
    )


def head_prepare(raw, gain, cosine, sine):
    head_width = gain.shape[0]
    shaped = raw.reshape(raw.shape[:-1] + (raw.shape[-1] // head_width, head_width))
    return rotate_halves(rms_scale(shaped, gain), cosine, sine)


def swiglu(gate, upper):
    return jax.nn.silu(gate) * upper


def contract(left, right, left_dim, right_dim):
    return lax.dot_general(
        left, right, (((left_dim,), (right_dim,)), ((), ())), preferred_element_type=jnp.float32
    )


def block_scores(query_block, keys, row_start):
    scale = 1.0 / query_block.shape[-1] ** 0.5
    scores = (
        jnp.einsum("qhd,khd->hqk", query_block, keys, preferred_element_type=jnp.float32) * scale
    )
    row_ids = row_start + jnp.arange(query_block.shape[0])
    col_ids = jnp.arange(keys.shape[0])
    allowed = col_ids[None, :] <= row_ids[:, None]
    return jnp.where(allowed[None, :, :], scores, -1e30)


def attend(queries, keys, values):
    length = queries.shape[0]
    block_rows = min(512, length)
    outputs = []
    totals = []
    for block_index in range(length // block_rows):
        start = block_index * block_rows
        scores = block_scores(queries[start : start + block_rows], keys, start)
        peak = jnp.max(scores, axis=-1, keepdims=True)
        log_total = peak + jnp.log(jnp.sum(jnp.exp(scores - peak), axis=-1, keepdims=True))
        probs = jnp.exp(scores - log_total).astype(jnp.bfloat16)
        block_out = jnp.einsum("hqk,khd->qhd", probs, values, preferred_element_type=jnp.float32)
        outputs.append(block_out.astype(jnp.bfloat16))
        totals.append(log_total[..., 0])
    return (jnp.concatenate(outputs, axis=0), jnp.concatenate(totals, axis=1))


def attend_grad(queries, keys, values, outputs, totals, out_grad):
    length = queries.shape[0]
    block_rows = min(512, length)
    scale = 1.0 / queries.shape[-1] ** 0.5
    key_acc = jnp.zeros(keys.shape, jnp.float32)
    value_acc = jnp.zeros(values.shape, jnp.float32)
    query_parts = []
    for block_index in range(length // block_rows):
        start = block_index * block_rows
        query_block = queries[start : start + block_rows]
        scores = block_scores(query_block, keys, start)
        probs = jnp.exp(scores - totals[:, start : start + block_rows][..., None])
        grad_block = out_grad[start : start + block_rows]
        value_acc = value_acc + jnp.einsum(
            "hqk,qhd->khd",
            probs.astype(jnp.bfloat16),
            grad_block,
            preferred_element_type=jnp.float32,
        )
        prob_grad = jnp.einsum(
            "qhd,khd->hqk", grad_block, values, preferred_element_type=jnp.float32
        )
        delta = jnp.sum(
            grad_block.astype(jnp.float32)
            * outputs[start : start + block_rows].astype(jnp.float32),
            axis=-1,
        ).T
        score_grad = (probs * (prob_grad - delta[..., None])).astype(jnp.bfloat16)
        query_parts.append(
            (
                jnp.einsum("hqk,khd->qhd", score_grad, keys, preferred_element_type=jnp.float32)
                * scale
            ).astype(jnp.bfloat16)
        )
        key_acc = (
            key_acc
            + jnp.einsum(
                "hqk,qhd->khd", score_grad, query_block, preferred_element_type=jnp.float32
            )
            * scale
        )
    return (
        jnp.concatenate(query_parts, axis=0),
        key_acc.astype(jnp.bfloat16),
        value_acc.astype(jnp.bfloat16),
    )


def shards(
    block_input,
    operator_gain,
    query_weight,
    key_weight,
    value_weight,
    output_weight,
    feedforward_gain,
    gate_weight,
    up_weight,
    down_weight,
    query_gain,
    key_gain,
    cotangent,
):
    gathered = (
        lax.all_gather(operator_gain, "fsdp", axis=0, tiled=True),
        lax.all_gather(query_weight, "fsdp", axis=0, tiled=True),
        lax.all_gather(key_weight, "fsdp", axis=0, tiled=True),
        lax.all_gather(value_weight, "fsdp", axis=0, tiled=True),
        lax.all_gather(output_weight, "fsdp", axis=1, tiled=True),
        lax.all_gather(feedforward_gain, "fsdp", axis=0, tiled=True),
        lax.all_gather(gate_weight, "fsdp", axis=0, tiled=True),
        lax.all_gather(up_weight, "fsdp", axis=0, tiled=True),
        lax.all_gather(down_weight, "fsdp", axis=1, tiled=True),
        lax.all_gather(query_gain, "fsdp", axis=0, tiled=True),
        lax.all_gather(key_gain, "fsdp", axis=0, tiled=True),
    )
    (
        operator_full,
        query_full,
        key_full,
        value_full,
        output_full,
        feedforward_full,
        gate_full,
        upper_full,
        down_full,
        query_gain_full,
        key_gain_full,
    ) = gathered
    operator_scale = operator_full.astype(jnp.float32)
    feedforward_scale = feedforward_full.astype(jnp.float32)
    query_scale = query_gain_full.astype(jnp.float32)
    key_scale = key_gain_full.astype(jnp.float32)
    seqs_here, tok_here, width = block_input.shape
    rows = seqs_here * tok_here
    head_width = query_scale.shape[0]
    heads_here = query_full.shape[1] // head_width
    kv_here = key_full.shape[1] // head_width
    group = heads_here // kv_here
    positions = lax.axis_index("ctx") * tok_here + jnp.arange(tok_here)
    cosine, sine = rotary_tables(positions, head_width)

    def prepare(raw, gain):
        return head_prepare(raw, gain, cosine, sine)

    input_flat = block_input.reshape(rows, width).astype(jnp.float32)
    norm_one, norm_one_back = jax.vjp(rms_scale, input_flat, operator_scale)
    normed_input = norm_one.astype(jnp.bfloat16)
    query_raw = jnp.dot(normed_input, query_full, preferred_element_type=jnp.float32).reshape(
        seqs_here, tok_here, -1
    )
    key_raw = jnp.dot(normed_input, key_full, preferred_element_type=jnp.float32).reshape(
        seqs_here, tok_here, -1
    )
    value_raw = jnp.dot(normed_input, value_full, preferred_element_type=jnp.float32)
    query_f32, query_back = jax.vjp(prepare, query_raw, query_scale)
    key_f32, key_back = jax.vjp(prepare, key_raw, key_scale)
    queries = query_f32.astype(jnp.bfloat16)
    keys = jnp.repeat(key_f32.astype(jnp.bfloat16), group, axis=2)
    values = jnp.repeat(
        value_raw.astype(jnp.bfloat16).reshape(seqs_here, tok_here, kv_here, head_width),
        group,
        axis=2,
    )
    packed = jnp.concatenate([queries, keys, values], axis=3)
    by_heads = lax.all_to_all(packed, "ctx", split_axis=2, concat_axis=1, tiled=True)
    head_query = by_heads[..., :head_width]
    head_key = by_heads[..., head_width : 2 * head_width]
    head_value = by_heads[..., 2 * head_width :]
    head_out, head_total = jax.vmap(attend)(head_query, head_key, head_value)
    back_tokens = jax.tree.map(
        lambda part, own: part.astype(own.dtype),
        lax.all_to_all(as_sent(head_out), "ctx", split_axis=1, concat_axis=2, tiled=True),
        head_out,
    )
    attended = back_tokens.reshape(rows, heads_here * head_width)
    attention_part = jnp.dot(attended, output_full, preferred_element_type=jnp.float32)
    hidden = input_flat + lax.psum(attention_part, "tensor")
    norm_two, norm_two_back = jax.vjp(rms_scale, hidden, feedforward_scale)
    normed_hidden = norm_two.astype(jnp.bfloat16)
    gate = jnp.dot(normed_hidden, gate_full, preferred_element_type=jnp.float32)
    upper = jnp.dot(normed_hidden, upper_full, preferred_element_type=jnp.float32)
    act_f32, act_back = jax.vjp(swiglu, gate, upper)
    activation = act_f32.astype(jnp.bfloat16)
    down_part = jnp.dot(activation, down_full, preferred_element_type=jnp.float32)
    output_f32 = hidden + lax.psum(down_part, "tensor")
    block_output = output_f32.astype(jnp.bfloat16).reshape(seqs_here, tok_here, width)
    upstream = cotangent.reshape(rows, width)
    down_grad = contract(activation, upstream, 0, 0)
    act_grad = contract(upstream, down_full, 1, 1)
    gate_grad, upper_grad = act_back(act_grad)
    gate_grad = gate_grad.astype(jnp.bfloat16)
    upper_grad = upper_grad.astype(jnp.bfloat16)
    gate_weight_grad = contract(normed_hidden, gate_grad, 0, 0)
    up_weight_grad = contract(normed_hidden, upper_grad, 0, 0)
    hidden_part = contract(gate_grad, gate_full, 1, 1) + contract(upper_grad, upper_full, 1, 1)
    normed_hidden_grad = lax.psum(hidden_part, "tensor")
    hidden_norm_grad, feedforward_gain_grad = norm_two_back(normed_hidden_grad)
    hidden_grad = upstream.astype(jnp.float32) + hidden_norm_grad
    hidden_grad_b = hidden_grad.astype(jnp.bfloat16)
    output_weight_grad = contract(attended, hidden_grad_b, 0, 0)
    attended_grad = (
        contract(hidden_grad_b, output_full, 1, 1)
        .astype(jnp.bfloat16)
        .reshape(seqs_here, tok_here, heads_here, head_width)
    )
    grad_heads = lax.all_to_all(attended_grad, "ctx", split_axis=2, concat_axis=1, tiled=True)
    head_qgrad, head_kgrad, head_vgrad = jax.vmap(attend_grad)(
        head_query, head_key, head_value, head_out, head_total, grad_heads
    )
    packed_grad = jnp.concatenate([head_qgrad, head_kgrad, head_vgrad], axis=3)
    token_grad = lax.all_to_all(
        as_sent(packed_grad), "ctx", split_axis=1, concat_axis=2, tiled=True
    ).astype(packed_grad.dtype)
    query_tgrad = token_grad[..., :head_width]
    key_tgrad = token_grad[..., head_width : 2 * head_width]
    value_tgrad = token_grad[..., 2 * head_width :]
    key_sum = (
        key_tgrad.astype(jnp.float32)
        .reshape(seqs_here, tok_here, kv_here, group, head_width)
        .sum(axis=3)
    )
    value_sum = (
        value_tgrad.astype(jnp.float32)
        .reshape(seqs_here, tok_here, kv_here, group, head_width)
        .sum(axis=3)
    )
    query_pre, query_gain_part = query_back(query_tgrad.astype(jnp.float32))
    key_pre, key_gain_part = key_back(key_sum)
    query_raw_grad = query_pre.astype(jnp.bfloat16).reshape(rows, heads_here * head_width)
    key_raw_grad = key_pre.astype(jnp.bfloat16).reshape(rows, kv_here * head_width)
    value_raw_grad = value_sum.astype(jnp.bfloat16).reshape(rows, kv_here * head_width)
    query_weight_grad = contract(normed_input, query_raw_grad, 0, 0)
    key_weight_grad = contract(normed_input, key_raw_grad, 0, 0)
    value_weight_grad = contract(normed_input, value_raw_grad, 0, 0)
    input_part = (
        contract(query_raw_grad, query_full, 1, 1)
        + contract(key_raw_grad, key_full, 1, 1)
        + contract(value_raw_grad, value_full, 1, 1)
    )
    normed_input_grad, query_gain_grad, key_gain_grad = lax.psum(
        (input_part, query_gain_part, key_gain_part), "tensor"
    )
    input_norm_grad, operator_gain_grad = norm_one_back(normed_input_grad)
    input_grad = (hidden_grad + input_norm_grad).reshape(seqs_here, tok_here, width)
    grads = (
        operator_gain_grad,
        query_weight_grad,
        key_weight_grad,
        value_weight_grad,
        output_weight_grad,
        feedforward_gain_grad,
        gate_weight_grad,
        up_weight_grad,
        down_grad,
        query_gain_grad,
        key_gain_grad,
    )
    shares = (
        lax.psum_scatter(grads[0], "fsdp", scatter_dimension=0, tiled=True),
        lax.psum_scatter(grads[1], "fsdp", scatter_dimension=0, tiled=True),
        lax.psum_scatter(grads[2], "fsdp", scatter_dimension=0, tiled=True),
        lax.psum_scatter(grads[3], "fsdp", scatter_dimension=0, tiled=True),
        lax.psum_scatter(grads[4], "fsdp", scatter_dimension=1, tiled=True),
        lax.psum_scatter(grads[5], "fsdp", scatter_dimension=0, tiled=True),
        lax.psum_scatter(grads[6], "fsdp", scatter_dimension=0, tiled=True),
        lax.psum_scatter(grads[7], "fsdp", scatter_dimension=0, tiled=True),
        lax.psum_scatter(grads[8], "fsdp", scatter_dimension=1, tiled=True),
        lax.psum_scatter(grads[9], "fsdp", scatter_dimension=0, tiled=True),
        lax.psum_scatter(grads[10], "fsdp", scatter_dimension=0, tiled=True),
    )
    shares = tuple(
        lax.psum(
            (
                shares[0],
                shares[1],
                shares[2],
                shares[3],
                shares[4],
                shares[5],
                shares[6],
                shares[7],
                shares[8],
                shares[9],
                shares[10],
            ),
            "ctx",
        )
    )
    return (block_output, input_grad) + shares


def solution(mesh):
    in_specs = (
        P("fsdp", "ctx", None),
        P("fsdp"),
        P("fsdp", "tensor"),
        P("fsdp", "tensor"),
        P("fsdp", "tensor"),
        P("tensor", "fsdp"),
        P("fsdp"),
        P("fsdp", "tensor"),
        P("fsdp", "tensor"),
        P("tensor", "fsdp"),
        P("fsdp"),
        P("fsdp"),
        P("fsdp", "ctx", None),
    )
    out_specs = (
        P("fsdp", "ctx", None),
        P("fsdp", "ctx", None),
        P("fsdp"),
        P("fsdp", "tensor"),
        P("fsdp", "tensor"),
        P("fsdp", "tensor"),
        P("tensor", "fsdp"),
        P("fsdp"),
        P("fsdp", "tensor"),
        P("fsdp", "tensor"),
        P("tensor", "fsdp"),
        P("fsdp"),
        P("fsdp"),
    )
    return jax.shard_map(shards, mesh=mesh, in_specs=in_specs, out_specs=out_specs, check_vma=False)
```

profile of v0, /device:TPU:0, one launch (start us, length us, event | category | flops | bytes accessed | tf_op | source)
XLA Modules:
  0.0 1489.3 jit_solution(11856030117197905531)
XLA Ops:
  7.9 22.5 %all-gather = bf16[8,1,128]{2,1,0:T(2,128)(2,1)S(1)} all-gather(bf16[1,1,128]{2,1,0:T(2,128)(2,1)} %bitcast.270), channel_id=1, replica_groups=mesh['fsdp'=8,'ctx'=2,'tensor'=2] {'fsdp'}, dimensions={0}, use_global_device_ids=true | all-gather | bytes 2304 | tf_op jit(solution)/shard_map/all_gather | solution.py:150
  32.0 32.4 %all_gather.36 = bf16[1024,256]{1,0:T(8,128)(2,1)S(1)} all-gather(bf16[128,256]{1,0:T(8,128)(2,1)} %param.16), channel_id=1, replica_groups=mesh['fsdp'=8,'ctx'=2,'tensor'=2] {'fsdp'}, dimensions={0}, use_global_device_ids=true | all-gather | bytes 589824 | tf_op jit(solution)/shard_map/all_gather | solution.py:152
  68.2 17.1 %all-reduce.15 = (bf16[64]{0:T(256)(128)(2,1)S(1)}, bf16[64]{0:T(256)(128)(2,1)S(1)}) all-reduce(bf16[64]{0:T(256)(128)(2,1)S(1)} %dynamic-update-slice.1, bf16[64]{0:T(256)(128)(2,1)S(1)} %dynamic-update-slice), channel_id=1, replica_groups=mesh['fsdp'=8,'ctx'=2,'tensor'=2] {'fsdp'}, use_global_device_ids=true, to_apply=%add.5 | all-reduce | flops 128 | bytes 512
  86.7 31.2 %all_gather.38 = bf16[1024,256]{1,0:T(8,128)(2,1)S(1)} all-gather(bf16[128,256]{1,0:T(8,128)(2,1)S(1)} %copy-done.42), channel_id=1, replica_groups=mesh['fsdp'=8,'ctx'=2,'tensor'=2] {'fsdp'}, dimensions={0}, use_global_device_ids=true | all-gather | bytes 589824 | tf_op jit(solution)/shard_map/all_gather | solution.py:153
  129.6 9.9 all-to-all-done
  157.1 9.4 all_to_all.69
  174.3 18.4 %all-gather.1 = bf16[8,1,128]{2,1,0:T(2,128)(2,1)S(1)} all-gather(bf16[1,1,128]{2,1,0:T(2,128)(2,1)S(1)} %bitcast.271), channel_id=1, replica_groups=mesh['fsdp'=8,'ctx'=2,'tensor'=2] {'fsdp'}, dimensions={0}, use_global_device_ids=true | all-gather | bytes 2304 | tf_op jit(solution)/shard_map/all_gather | solution.py:155
  197.8 77.7 %all-gather.12.cloned.1.call-done = bf16[1024,2304]{1,0:T(8,128)(2,1)} async-done(((bf16[128,2304]{1,0:T(8,128)(2,1)}), bf16[1024,2304]{1,0:T(8,128)(2,1)}) %all-gather.12.cloned.1.call-update) | async-done | bytes 4718608 | tf_op jit(solution)/shard_map/all_gather | solution.py:156
  283.0 72.3 %all-gather.14.cloned.1.call-done = bf16[1024,2304]{1,0:T(8,128)(2,1)} async-done(((bf16[128,2304]{1,0:T(8,128)(2,1)}), bf16[1024,2304]{1,0:T(8,128)(2,1)}) %all-gather.14.cloned.1.call-update) | async-done | bytes 4718608 | tf_op jit(solution)/shard_map/all_gather | solution.py:157
  362.7 73.5 %all-gather.16.cloned.1.call-done = bf16[2304,1024]{1,0:T(8,128)(2,1)} async-done(((bf16[2304,128]{1,0:T(8,128)(2,1)}), bf16[2304,1024]{1,0:T(8,128)(2,1)}) %all-gather.16.cloned.1.call-update) | async-done | bytes 4718608 | tf_op jit(solution)/shard_map/all_gather | solution.py:158
  436.2 11.2 multiply_convert_fusion.2
  457.9 19.4 %all-reduce.23.cloned.1.call-done = f32[512,1024]{1,0:T(8,128)} async-done(((f32[512,1024]{1,0:T(8,128)}), f32[512,1024]{1,0:T(8,128)}) %all-reduce.23.cloned.1.call-update) | async-done | bytes 2097168 | tf_op jit(solution)/shard_map/psum | solution.py:242
  483.6 11.2 all_to_all.70
  516.7 30.3 %all_to_all.71 = bf16[1,1024,4,192]{3,2,0,1:T(4,128)(2,1)} all-to-all(bf16[1,1024,4,192]{3,2,0,1:T(4,128)(2,1)} %copy.51), channel_id=1, replica_groups=mesh['fsdp'=8,'ctx'=2,'tensor'=2] {'ctx'}, dimensions={1} | all-to-all | bytes 3145728 | tf_op jit(solution)/shard_map/all_to_all | solution.py:257
  605.0 17.1 %reduce-scatter.10.cloned.1.call-done = f32[128,256]{1,0:T(8,128)} async-done(((f32[1024,256]{1,0:T(8,128)}), f32[128,256]{1,0:T(8,128)}) %reduce-scatter.10.cloned.1.call-update) | async-done | bytes 131088 | tf_op jit(solution)/shard_map/reduce_scatter | solution.py:307
  622.1 67.1 %reduce-scatter.12.cloned.1.call-done = f32[128,256]{1,0:T(8,128)} async-done(((f32[1024,256]{1,0:T(8,128)}), f32[128,256]{1,0:T(8,128)}) %reduce-scatter.12.cloned.1.call-update) | async-done | bytes 131088 | tf_op jit(solution)/shard_map/reduce_scatter | solution.py:308
  689.2 71.6 %reduce-scatter.14.cloned.1.call-done = f32[512,128]{1,0:T(8,128)} async-done(((f32[512,1024]{1,0:T(8,128)}), f32[512,128]{1,0:T(8,128)}) %reduce-scatter.14.cloned.1.call-update) | async-done | bytes 262160 | tf_op jit(solution)/shard_map/reduce_scatter | solution.py:309
  760.8 71.0 %reduce-scatter.8.cloned.1.call-done = f32[128,512]{1,0:T(8,128)} async-done(((f32[1024,512]{1,0:T(8,128)}), f32[128,512]{1,0:T(8,128)}) %reduce-scatter.8.cloned.1.call-update) | async-done | bytes 262160 | tf_op jit(solution)/shard_map/reduce_scatter | solution.py:306
  831.8 164.7 %reduce-scatter.16.cloned.1.call-done = f32[128,2304]{1,0:T(8,128)} async-done(((f32[1024,2304]{1,0:T(8,128)}), f32[128,2304]{1,0:T(8,128)}) %reduce-scatter.16.cloned.1.call-update) | async-done | bytes 1179664 | tf_op jit(solution)/shard_map/reduce_scatter | solution.py:311
  996.5 164.8 %reduce-scatter.18.cloned.1.call-done = f32[128,2304]{1,0:T(8,128)} async-done(((f32[1024,2304]{1,0:T(8,128)}), f32[128,2304]{1,0:T(8,128)}) %reduce-scatter.18.cloned.1.call-update) | async-done | bytes 1179664 | tf_op jit(solution)/shard_map/reduce_scatter | solution.py:312
  1161.3 165.1 %reduce-scatter.20.cloned.1.call-done = f32[2304,128]{1,0:T(8,128)} async-done(((f32[2304,1024]{1,0:T(8,128)}), f32[2304,128]{1,0:T(8,128)}) %reduce-scatter.20.cloned.1.call-update) | async-done | bytes 1179664 | tf_op jit(solution)/shard_map/reduce_scatter | solution.py:313
  1327.1 29.2 %all-reduce.25.cloned.1.call-done = (f32[512,1024]{1,0:T(8,128)}, f32[512,1024]{1,0:T(8,128)}) async-done(((f32[512,1024]{1,0:T(8,128)}, f32[512,1024]{1,0:T(8,128)}), (f32[512,1024]{1,0:T(8,128)}, f32[512,1024]{1,0:T(8,128)})) %all-reduce.25.cloned.1.call-update) | async-done | bytes 4194320 | tf_op jit(solution)/shard_map/psum | solution.py:231
  1358.7 22.1 %all-reduce.10 = (f32[1024]{0:T(1024)S(1)}, f32[1024]{0:T(1024)S(1)}, f32[64]{0:T(128)S(1)}, f32[64]{0:T(128)S(1)}) all-reduce(f32[1024]{0:T(1024)S(1)} %get-tuple-element.15, f32[1024]{0:T(1024)S(1)} %copy-done.55, f32[64]{0:T(128)S(1)} %get-tuple-element.19, ...), channel_id=2, replica_groups=mesh['fsdp'=8,'ctx'=2,'tensor'=2] {'fsdp'}, use_global_device_ids=true, to_apply=%region_21.22.clone | all-reduce | flops 2176 | bytes 17408
  1395.3 76.1 %all-reduce.27.cloned.1.call-done = (f32[128,512]{1,0:T(8,128)}, f32[128,256]{1,0:T(8,128)}, f32[128,256]{1,0:T(8,128)}, f32[512,128]{1,0:T(8,128)}, f32[128,230...) async-done(((f32[128,512]{1,0:T(8,128)}, f32[128,256]{1,0:T(8,128)}, f32[128,256]{1,0:T(8,128)}, f32[512,128]{1,0:T(8,128)}, f32[128,2304]{1,0:T(8,128)}, ...) | async-done | bytes 4325392 | tf_op jit(solution)/shard_map/psum | solution.py:318
  (300 shorter events, 186.6 us)
Async XLA Ops:
  7.2 59.3 %copy-start.65 = (u32[32]{0:T(128)S(1)}, u32[32]{0:T(128)}, u32[]{:S(2)}) copy-start(u32[32]{0:T(128)} %constant.61) | copy-start | bytes 388
  7.2 60.5 %copy-start.68 = (bf16[8]{0:T(256)(128)(2,1)S(1)}, bf16[8]{0:T(256)(128)(2,1)}, u32[]{:S(2)}) copy-start(bf16[8]{0:T(256)(128)(2,1)} %param.24) | copy-start | bytes 52
  7.2 60.8 %copy-start.69 = (bf16[8]{0:T(256)(128)(2,1)S(1)}, bf16[8]{0:T(256)(128)(2,1)}, u32[]{:S(2)}) copy-start(bf16[8]{0:T(256)(128)(2,1)} %param.23) | copy-start | bytes 52
  7.2 112.0 %all-gather.8.cloned.1.call-start = ((), (), s32[]{:S(2)}) async-start(), calls=%async_computation.11 | async-start | bytes 1179648 | tf_op jit(solution)/shard_map/all_gather | solution.py:151
  30.4 88.8 %copy-start.43 = (f32[8,1,128]{2,1,0:T(1,128)}, f32[8,1,128]{2,1,0:T(1,128)S(1)}, u32[]{:S(2)}) copy-start(f32[8,1,128]{2,1,0:T(1,128)S(1)} %convert_element_type.269) | copy-start | bytes 12292
  31.9 87.3 %copy-start.48 = (f32[512]{0:T(512)}, f32[512]{0:T(512)S(1)}, u32[]{:S(2)}) copy-start(f32[512]{0:T(512)S(1)} %fusion.62) | copy-start | bytes 6148
  123.6 15.9 %all-to-all-start = ((bf16[1,512,8,192]{1,3,0,2:T(8,128)(2,1)}), bf16[1,512,8,192]{1,3,0,2:T(8,128)(2,1)S(1)}, u32[]{:S(2)}, u32[]{:S(2)}) async-start(bf16[1,512,8,192]{1,3,0,2:T(8,128)(2,1)} %pad_maximum_fusion), calls=%async_computation | async-start | bytes 3145728 | tf_op jit(solution)/shard_map/all_to_all | solution.py:211
  127.3 41.9 %all-gather.10.cloned.1.call-start = ((), (), s32[]{:S(2)}) async-start(), calls=%async_computation.12 | async-start | bytes 1179648 | tf_op jit(solution)/shard_map/all_gather | solution.py:154
  128.0 65.2 %all-reduce.21.cloned.1.call-start = ((), (), s32[]{:S(2)}) async-start(), calls=%async_computation.13 | async-start | bytes 4194304 | tf_op jit(solution)/shard_map/psum | solution.py:223
  172.5 103.0 %all-gather.12.cloned.1.call-start = ((), (), s32[]{:S(2)}) async-start(), calls=%async_computation.14 | async-start | bytes 5308416 | tf_op jit(solution)/shard_map/all_gather | solution.py:156
  173.1 182.2 %all-gather.14.cloned.1.call-start = ((), (), s32[]{:S(2)}) async-start(), calls=%async_computation.15 | async-start | bytes 5308416 | tf_op jit(solution)/shard_map/all_gather | solution.py:157
  173.7 262.5 %all-gather.16.cloned.1.call-start = ((), (), s32[]{:S(2)}) async-start(), calls=%async_computation.16 | async-start | bytes 5308416 | tf_op jit(solution)/shard_map/all_gather | solution.py:158
  174.2 303.0 %all-reduce.23.cloned.1.call-start = ((), (), s32[]{:S(2)}) async-start(), calls=%async_computation.17 | async-start | bytes 4194304 | tf_op jit(solution)/shard_map/psum | solution.py:242
  457.7 164.4 %reduce-scatter.10.cloned.1.call-start = ((), (), s32[]{:S(2)}) async-start(), calls=%async_computation.19 | async-start | bytes 1179648 | tf_op jit(solution)/shard_map/reduce_scatter | solution.py:307
  557.4 131.8 %reduce-scatter.12.cloned.1.call-start = ((), (), s32[]{:S(2)}) async-start(), calls=%async_computation.20 | async-start | bytes 1179648 | tf_op jit(solution)/shard_map/reduce_scatter | solution.py:308
  561.4 199.4 %reduce-scatter.14.cloned.1.call-start = ((), (), s32[]{:S(2)}) async-start(), calls=%async_computation.21 | async-start | bytes 2359296 | tf_op jit(solution)/shard_map/reduce_scatter | solution.py:309
  565.3 266.4 %reduce-scatter.8.cloned.1.call-start = ((), (), s32[]{:S(2)}) async-start(), calls=%async_computation.18 | async-start | bytes 2359296 | tf_op jit(solution)/shard_map/reduce_scatter | solution.py:306
  571.5 424.9 %reduce-scatter.16.cloned.1.call-start = ((), (), s32[]{:S(2)}) async-start(), calls=%async_computation.22 | async-start | bytes 10616832 | tf_op jit(solution)/shard_map/reduce_scatter | solution.py:311
  578.5 582.8 %reduce-scatter.18.cloned.1.call-start = ((), (), s32[]{:S(2)}) async-start(), calls=%async_computation.23 | async-start | bytes 10616832 | tf_op jit(solution)/shard_map/reduce_scatter | solution.py:312
  585.3 741.2 %reduce-scatter.20.cloned.1.call-start = ((), (), s32[]{:S(2)}) async-start(), calls=%async_computation.24 | async-start | bytes 10616832 | tf_op jit(solution)/shard_map/reduce_scatter | solution.py:313
  593.3 763.0 %all-reduce.25.cloned.1.call-start = ((), (), s32[]{:S(2)}) async-start(), calls=%async_computation.25 | async-start | bytes 8388608 | tf_op jit(solution)/shard_map/psum | solution.py:231
  604.9 751.4 %copy-start.4 = (bf16[1,512,1024]{2,1,0:T(8,128)(2,1)S(1)}, bf16[1,512,1024]{2,1,0:T(8,128)(2,1)}, u32[]{:S(2)}) copy-start(bf16[1,512,1024]{2,1,0:T(8,128)(2,1)} %param.13) | copy-start | bytes 3145732
  604.9 866.5 %all-reduce.27.cloned.1.call-start = ((), (), s32[]{:S(2)}) async-start(), calls=%async_computation.26 | async-start | bytes 8650752 | tf_op jit(solution)/shard_map/psum | solution.py:318
  1326.5 63.4 %copy-start.52 = (f32[512]{0:T(512)S(1)}, f32[512]{0:T(512)}, u32[]{:S(2)}) copy-start(f32[512]{0:T(512)} %copy-done.51) | copy-start | bytes 6148
  (69 other events, 504.2 us)
Sparse Core Ops, SparseCore 0:
  10.1 45.4 all-gather.7
  130.1 38.9 all-gather.9
  172.6 20.2 all-reduce.20
  195.0 80.4 all-gather.11
  277.6 77.6 all-gather.13
  357.2 78.9 all-gather.15
  457.8 19.4 all-reduce.22
  557.5 64.5 reduce-scatter.9
  626.1 63.0 reduce-scatter.11
  692.6 68.1 reduce-scatter.13
  764.3 67.3 reduce-scatter.7
  835.2 161.2 reduce-scatter.15
  1000.1 161.2 reduce-scatter.17
  1164.8 161.6 reduce-scatter.19
  1328.8 27.4 all-reduce.24
  1359.3 112.0 all-reduce.26
where the time goes:
time: 1490 us
  waiting for transfers between devices  1080 us (72%)
  blocking collectives  203 us (14%)
  matrix products  111 us (7%)
  other arithmetic  37.3 us (3%)
  local copies, waits for them, and re-layouts  32.7 us (2%)
  between operations  17.3 us (1%)
    reduce_scatter x1, waiting for transfers between devices, shards(): lax.psum_scatter(grads[8], 'fsdp', scatter_dimension=1, tiled=True)  165 us
    reduce_scatter x1, waiting for transfers between devices, shards(): lax.psum_scatter(grads[7], 'fsdp', scatter_dimension=0, tiled=True)  165 us
    reduce_scatter x1, waiting for transfers between devices, shards(): lax.psum_scatter(grads[6], 'fsdp', scatter_dimension=0, tiled=True)  165 us
    all_gather x1, waiting for transfers between devices, shards(): lax.all_gather(gate_weight, 'fsdp', axis=0, tiled=True)  77.7 us
    psum x1, waiting for transfers between devices, shards(): lax.psum((shares[0], shares[1], shares[2], shares[3], shares[4], shares[5...  76.1 us
    all_gather x1, waiting for transfers between devices, shards(): lax.all_gather(down_weight, 'fsdp', axis=1, tiled=True)  73.5 us
    all_gather x1, waiting for transfers between devices, shards(): lax.all_gather(up_weight, 'fsdp', axis=0, tiled=True)  72.3 us
    reduce_scatter x1, waiting for transfers between devices, shards(): lax.psum_scatter(grads[4], 'fsdp', scatter_dimension=1, tiled=True)  71.6 us
  transfers between devices with their start and end apart: 17, of which 15 were waited for; matrix products, arithmetic and copies ran while one was open for 6% of the time, Pallas kernels for 0%

commit v1 on v0

v1 whole, which is shorter than its diff:
```python
import jax
import jax.numpy as jnp
from jax import lax
from jax.sharding import PartitionSpec as P

EPS = 1e-05
THETA = 1000000.0


def rms_scale(values_in, gain):
    return (
        values_in * lax.rsqrt(jnp.mean(values_in * values_in, axis=-1, keepdims=True) + EPS) * gain
    )


def rotary_tables(positions, head_width):
    half_width = head_width // 2
    freqs = THETA ** (-jnp.arange(half_width).astype(jnp.float32) * 2.0 / head_width)
    angles = positions.astype(jnp.float32)[:, None] * freqs[None, :]
    return (jnp.cos(angles), jnp.sin(angles))


def rotate_halves(heads_in, cosine, sine):
    half_width = heads_in.shape[-1] // 2
    front_half = heads_in[..., :half_width]
    back_half = heads_in[..., half_width:]
    cos_rows = cosine[:, None, :]
    sin_rows = sine[:, None, :]
    return jnp.concatenate(
        [
            front_half * cos_rows - back_half * sin_rows,
            back_half * cos_rows + front_half * sin_rows,
        ],
        axis=-1,
    )


def head_prepare(raw, gain, cosine, sine):
    head_width = gain.shape[0]
    shaped = raw.reshape(raw.shape[:-1] + (raw.shape[-1] // head_width, head_width))
    return rotate_halves(rms_scale(shaped, gain), cosine, sine)


def swiglu(gate, upper):
    return jax.nn.silu(gate) * upper


def contract(left, right, left_dim, right_dim):
    return lax.dot_general(
        left, right, (((left_dim,), (right_dim,)), ((), ())), preferred_element_type=jnp.float32
    )


def block_scores(query_block, keys, query_pos, key_pos):
    scale = 1.0 / query_block.shape[-1] ** 0.5
    scores = (
        jnp.einsum("qhd,khd->hqk", query_block, keys, preferred_element_type=jnp.float32) * scale
    )
    allowed = key_pos[None, :] <= query_pos[:, None]
    return jnp.where(allowed[None, :, :], scores, -1e30)


def attend(queries, keys, values, positions):
    length = queries.shape[0]
    block_rows = min(512, length)
    outputs = []
    totals = []
    for start in range(0, length, block_rows):
        rows = slice(start, start + block_rows)
        scores = block_scores(queries[rows], keys, positions[rows], positions)
        peak = jnp.max(scores, axis=-1, keepdims=True)
        log_total = peak + jnp.log(jnp.sum(jnp.exp(scores - peak), axis=-1, keepdims=True))
        probs = jnp.exp(scores - log_total).astype(jnp.bfloat16)
        block_out = jnp.einsum("hqk,khd->qhd", probs, values, preferred_element_type=jnp.float32)
        outputs.append(block_out.astype(jnp.bfloat16))
        totals.append(log_total[..., 0])
    return (jnp.concatenate(outputs, axis=0), jnp.concatenate(totals, axis=1))


def attend_grad(queries, keys, values, outputs, totals, out_grad, positions):
    length = queries.shape[0]
    block_rows = min(512, length)
    scale = 1.0 / queries.shape[-1] ** 0.5
    key_acc = jnp.zeros(keys.shape, jnp.float32)
    value_acc = jnp.zeros(values.shape, jnp.float32)
    query_parts = []
    for start in range(0, length, block_rows):
        rows = slice(start, start + block_rows)
        query_block = queries[rows]
        scores = block_scores(query_block, keys, positions[rows], positions)
        probs = jnp.exp(scores - totals[:, rows][..., None])
        grad_block = out_grad[rows]
        value_acc = value_acc + jnp.einsum(
            "hqk,qhd->khd",
            probs.astype(jnp.bfloat16),
            grad_block,
            preferred_element_type=jnp.float32,
        )
        prob_grad = jnp.einsum(
            "qhd,khd->hqk", grad_block, values, preferred_element_type=jnp.float32
        )
        delta = jnp.sum(
            grad_block.astype(jnp.float32) * outputs[rows].astype(jnp.float32),
            axis=-1,
        ).T
        score_grad = (probs * (prob_grad - delta[..., None])).astype(jnp.bfloat16)
        query_parts.append(
            (
                jnp.einsum("hqk,khd->qhd", score_grad, keys, preferred_element_type=jnp.float32)
                * scale
            ).astype(jnp.bfloat16)
        )
        key_acc = (
            key_acc
            + jnp.einsum(
                "hqk,qhd->khd", score_grad, query_block, preferred_element_type=jnp.float32
            )
            * scale
        )
    return (
        jnp.concatenate(query_parts, axis=0),
        key_acc.astype(jnp.bfloat16),
        value_acc.astype(jnp.bfloat16),
    )


def shift(array, axis_name, step):
    size = lax.axis_size(axis_name)
    return lax.ppermute(array, axis_name, [(i, (i + step) % size) for i in range(size)])


def around(array, axis_name, dim):
    size = lax.axis_size(axis_name)
    return jnp.concatenate(
        [array] + [shift(array, axis_name, step) for step in range(1, size)], axis=dim
    )


def group_rows(array):
    return around(around(array, "ctx", 1), "tensor", 1)


def sum_around(array, axis_name):
    size = lax.axis_size(axis_name)
    part = array.shape[1] // size
    total = array[:, :part].astype(jnp.float32)
    for step in range(1, size):
        piece = array[:, step * part : (step + 1) * part].astype(jnp.bfloat16)
        total = total + shift(piece, axis_name, -step).astype(jnp.float32)
    return total


def group_sum(array):
    return sum_around(sum_around(array, "tensor"), "ctx")


def in_order(array, axis_name, dim):
    size = lax.axis_size(axis_name)
    me = lax.axis_index(axis_name)
    width = array.shape[dim]
    shape = list(array.shape)
    shape[dim] = width * size
    out = jnp.zeros(shape, array.dtype)
    for step in range(size):
        piece = array if step == 0 else shift(array, axis_name, step)
        owner = lax.rem(me - step + size, size)
        out = lax.dynamic_update_slice_in_dim(out, piece, owner * width, dim)
    return out


def part_of(array, dim, count, start):
    return lax.dynamic_slice_in_dim(array, start, count, dim)


def shards(
    block_input,
    operator_gain,
    query_weight,
    key_weight,
    value_weight,
    output_weight,
    feedforward_gain,
    gate_weight,
    up_weight,
    down_weight,
    query_gain,
    key_gain,
    cotangent,
):
    bf16 = jnp.bfloat16
    f32 = jnp.float32
    fsdp = lax.axis_size("fsdp")
    ctx = lax.axis_size("ctx")
    tensor = lax.axis_size("tensor")
    me_f = lax.axis_index("fsdp")
    me_c = lax.axis_index("ctx")
    me_t = lax.axis_index("tensor")
    seqs, tok_here, width = block_input.shape
    quarter = tok_here // tensor
    tokens = tok_here * ctx
    rows = seqs * tokens
    gain_rows = query_gain.shape[0]
    head_width = gain_rows * fsdp
    heads_shard = query_weight.shape[1] // head_width
    kv_shard = key_weight.shape[1] // head_width
    spread = heads_shard // kv_shard
    heads = heads_shard // ctx
    kv = max(1, kv_shard // ctx)
    group = heads // kv
    copies = max(1, ctx // kv_shard)
    q_cols = heads * head_width
    kv_cols = kv * head_width
    kv_start = ((me_c * heads) // spread) * head_width
    hidden_units = gate_weight.shape[1] // ctx
    shard_rows = query_weight.shape[0]

    gains = jnp.stack(
        [
            operator_gain,
            feedforward_gain,
            jnp.pad(query_gain, (0, shard_rows - gain_rows)),
            jnp.pad(key_gain, (0, shard_rows - gain_rows)),
        ],
        axis=1,
    )
    attention_pack = jnp.concatenate(
        [
            part_of(query_weight, 1, q_cols, me_c * q_cols),
            part_of(key_weight, 1, kv_cols, kv_start),
            part_of(value_weight, 1, kv_cols, kv_start),
            part_of(output_weight, 0, q_cols, me_c * q_cols).T,
            jnp.pad(gains, ((0, 0), (0, 124))),
        ],
        axis=1,
    )
    gate_up_pack = jnp.concatenate(
        [
            part_of(gate_weight, 1, hidden_units, me_c * hidden_units),
            part_of(up_weight, 1, hidden_units, me_c * hidden_units),
        ],
        axis=1,
    )
    down_pack = part_of(down_weight, 0, hidden_units, me_c * hidden_units).T
    attention_full = lax.all_gather(attention_pack, "fsdp", axis=0, tiled=True)
    gate_up_full = lax.all_gather(gate_up_pack, "fsdp", axis=0, tiled=True)
    down_full = lax.all_gather(down_pack, "fsdp", axis=0, tiled=True)
    qkv_cols = q_cols + 2 * kv_cols
    qkv_full = attention_full[:, :qkv_cols]
    output_full = attention_full[:, qkv_cols : qkv_cols + q_cols]
    gains_full = attention_full[:, qkv_cols + q_cols :].astype(f32)
    operator_scale = gains_full[:, 0]
    feedforward_scale = gains_full[:, 1]
    query_scale = gains_full[:, 2].reshape(fsdp, shard_rows)[:, :gain_rows].reshape(-1)
    key_scale = gains_full[:, 3].reshape(fsdp, shard_rows)[:, :gain_rows].reshape(-1)

    own_input = part_of(block_input, 1, quarter, me_t * quarter)
    all_input = group_rows(own_input).reshape(rows, width)
    upstream_own = part_of(cotangent, 1, quarter, me_t * quarter)
    upstream = group_rows(upstream_own).reshape(rows, width)

    ctx_order = lax.rem(me_c - jnp.arange(ctx) + ctx, ctx)
    tensor_order = lax.rem(me_t - jnp.arange(tensor) + tensor, tensor)
    positions = (
        tensor_order[:, None, None] * quarter
        + ctx_order[None, :, None] * tok_here
        + jnp.arange(quarter)[None, None, :]
    ).reshape(tokens)
    cosine, sine = rotary_tables(positions, head_width)

    def prepare(raw, gain):
        return head_prepare(raw, gain, cosine, sine)

    normed_input = rms_scale(all_input.astype(f32), operator_scale).astype(bf16)
    qkv_raw = jnp.dot(normed_input, qkv_full, preferred_element_type=f32).reshape(seqs, tokens, -1)
    query_f32, query_back = jax.vjp(prepare, qkv_raw[..., :q_cols], query_scale)
    key_f32, key_back = jax.vjp(prepare, qkv_raw[..., q_cols : q_cols + kv_cols], key_scale)
    queries = query_f32.astype(bf16)
    keys = jnp.repeat(key_f32.astype(bf16), group, axis=2)
    values = jnp.repeat(
        qkv_raw[..., q_cols + kv_cols :].astype(bf16).reshape(seqs, tokens, kv, head_width),
        group,
        axis=2,
    )
    attended, totals = jax.vmap(attend, in_axes=(0, 0, 0, None))(queries, keys, values, positions)
    attended_rows = attended.reshape(rows, q_cols)
    attention_part = contract(attended_rows, output_full, 1, 1).reshape(seqs, tokens, width)
    own_f32 = own_input.astype(f32)
    hidden = own_f32 + group_sum(attention_part)
    norm_two, norm_two_back = jax.vjp(rms_scale, hidden, feedforward_scale)
    normed_hidden = group_rows(norm_two.astype(bf16)).reshape(rows, width)
    gate_up = jnp.dot(normed_hidden, gate_up_full, preferred_element_type=f32)
    act_f32, act_back = jax.vjp(swiglu, gate_up[:, :hidden_units], gate_up[:, hidden_units:])
    activation = act_f32.astype(bf16)
    act_grad = jnp.dot(upstream, down_full, preferred_element_type=f32)
    gate_grad, up_grad = act_back(act_grad)
    gate_up_grad = jnp.concatenate([gate_grad.astype(bf16), up_grad.astype(bf16)], axis=1)
    hidden_part = contract(gate_up_grad, gate_up_full, 1, 1).reshape(seqs, tokens, width)
    normed_hidden_grad = group_sum(hidden_part)
    down_grad = contract(upstream, activation, 0, 0).astype(bf16)
    down_share = lax.psum_scatter(down_grad, "fsdp", scatter_dimension=0, tiled=True)
    gate_up_weight_grad = contract(normed_hidden, gate_up_grad, 0, 0).astype(bf16)
    gate_up_share = lax.psum_scatter(gate_up_weight_grad, "fsdp", scatter_dimension=0, tiled=True)
    down_part = contract(activation, down_full, 1, 1).reshape(seqs, tokens, width)
    own_output = (hidden + group_sum(down_part)).astype(bf16)
    block_output = in_order(own_output, "tensor", 1)

    hidden_norm_grad, feedforward_gain_grad = norm_two_back(normed_hidden_grad)
    hidden_grad = upstream_own.astype(f32) + hidden_norm_grad
    hidden_grad_b = group_rows(hidden_grad.astype(bf16)).reshape(rows, width)
    output_weight_grad = contract(hidden_grad_b, attended_rows, 0, 0)
    attended_grad = (
        jnp.dot(hidden_grad_b, output_full, preferred_element_type=f32)
        .astype(bf16)
        .reshape(seqs, tokens, heads, head_width)
    )
    query_hgrad, key_hgrad, value_hgrad = jax.vmap(attend_grad, in_axes=(0, 0, 0, 0, 0, 0, None))(
        queries, keys, values, attended, totals, attended_grad, positions
    )

    def head_sum(grad):
        return grad.astype(f32).reshape(seqs, tokens, kv, group, head_width).sum(axis=3)

    query_pre, query_gain_grad = query_back(query_hgrad.astype(f32))
    key_pre, key_gain_grad = key_back(head_sum(key_hgrad))
    qkv_raw_grad = jnp.concatenate(
        [
            query_pre.astype(bf16).reshape(rows, q_cols),
            key_pre.astype(bf16).reshape(rows, kv_cols),
            head_sum(value_hgrad).astype(bf16).reshape(rows, kv_cols),
        ],
        axis=1,
    )
    input_part = contract(qkv_raw_grad, qkv_full, 1, 1).reshape(seqs, tokens, width)
    normed_input_grad = group_sum(input_part)
    qkv_weight_grad = contract(normed_input, qkv_raw_grad, 0, 0)
    attention_grad = jnp.concatenate([qkv_weight_grad, output_weight_grad], axis=1).astype(bf16)
    attention_share = lax.psum_scatter(attention_grad, "fsdp", scatter_dimension=0, tiled=True)
    _, norm_one_back = jax.vjp(rms_scale, own_f32, operator_scale)
    input_norm_grad, operator_gain_grad = norm_one_back(normed_input_grad)
    input_grad = in_order(hidden_grad + input_norm_grad, "tensor", 1)

    gain_sums = lax.psum(
        jnp.concatenate([operator_gain_grad, feedforward_gain_grad, query_gain_grad, key_gain_grad]),
        ("fsdp", "ctx", "tensor"),
    )
    operator_share = part_of(gain_sums, 0, shard_rows, me_f * shard_rows)
    feedforward_share = part_of(gain_sums, 0, shard_rows, width + me_f * shard_rows)
    query_gain_share = part_of(gain_sums, 0, gain_rows, 2 * width + me_f * gain_rows)
    key_gain_share = part_of(gain_sums, 0, gain_rows, 2 * width + head_width + me_f * gain_rows)

    def spread_cols(share):
        return in_order(share, "ctx", 1).astype(f32)

    def spread_heads(share):
        if copies == 1:
            return spread_cols(share)
        every = in_order(share, "ctx", 1).astype(f32)
        return every.reshape(shard_rows, kv_shard, copies, head_width).sum(axis=2).reshape(
            shard_rows, -1
        )

    return (
        block_output,
        input_grad,
        operator_share,
        spread_cols(attention_share[:, :q_cols]),
        spread_heads(attention_share[:, q_cols : q_cols + kv_cols]),
        spread_heads(attention_share[:, q_cols + kv_cols : qkv_cols]),
        in_order(attention_share[:, qkv_cols:].T, "ctx", 0).astype(f32),
        feedforward_share,
        spread_cols(gate_up_share[:, :hidden_units]),
        spread_cols(gate_up_share[:, hidden_units:]),
        in_order(down_share.T, "ctx", 0).astype(f32),
        query_gain_share,
        key_gain_share,
    )


def solution(mesh):
    in_specs = (
        P("fsdp", "ctx", None),
        P("fsdp"),
        P("fsdp", "tensor"),
        P("fsdp", "tensor"),
        P("fsdp", "tensor"),
        P("tensor", "fsdp"),
        P("fsdp"),
        P("fsdp", "tensor"),
        P("fsdp", "tensor"),
        P("tensor", "fsdp"),
        P("fsdp"),
        P("fsdp"),
        P("fsdp", "ctx", None),
    )
    out_specs = (
        P("fsdp", "ctx", None),
        P("fsdp", "ctx", None),
        P("fsdp"),
        P("fsdp", "tensor"),
        P("fsdp", "tensor"),
        P("fsdp", "tensor"),
        P("tensor", "fsdp"),
        P("fsdp"),
        P("fsdp", "tensor"),
        P("fsdp", "tensor"),
        P("tensor", "fsdp"),
        P("fsdp"),
        P("fsdp"),
    )
    return jax.shard_map(shards, mesh=mesh, in_specs=in_specs, out_specs=out_specs, check_vma=False)
```

time: 1490 us -> 516 us (0.35)
  waiting for transfers between devices: 1080 us -> 264 us
  blocking collectives: 203 us -> 40.7 us
  matrix products: 111 us -> 89.8 us
  starting transfers between devices: 4.93 us -> 22.3 us
    reduce_scatter x7 -> x2, waiting for transfers between devices: 721 us -> 80.4 us  [the longest x1 80.4 us: shards(): lax.psum_scatter(gate_up_weight_grad, 'fsdp', scatter_dimension=0, tiled=...]
    all_gather x5 -> x3, waiting for transfers between devices: 224 us -> 74.1 us  [the longest x1 42.4 us: shards(): down_full = lax.all_gather(down_pack, 'fsdp', axis=0, tiled=True)]
    psum x4 -> x0, waiting for transfers between devices: 125 us -> none  [the longest x1 76.1 us: shards(): lax.psum((shares[0], shares[1], shares[2], shares[3], shares[4], shares[5...]
    ppermute x0 -> x25, waiting for transfers between devices: none -> 109 us  [shift(): lax.ppermute(array, axis_name, [(i, (i + step) % size) for i in range(siz...]
    all_gather x4 -> x0, blocking collectives: 104 us -> none  [the longest x1 32.4 us: shards(): lax.all_gather(key_weight, 'fsdp', axis=0, tiled=True)]
    all_to_all x3 -> x0, blocking collectives: 50.9 us -> none  [the longest x1 30.3 us: shards(): lax.all_to_all(as_sent(packed_grad), 'ctx', split_axis=1, concat_axis=2,...]
    unnamed x2 -> x0, blocking collectives: 39.3 us -> none
    psum x2 -> x1, blocking collectives: 8.11 us -> 40.7 us  [shards(): lax.psum(jnp.concatenate([operator_gain_grad, feedforward_gain_grad, quer...]
  transfers between devices with their start and end apart: 17 -> 31, of which waited for: 15 -> 19; matrix products, arithmetic and copies ran while one was open for 6% -> 26% of each run, Pallas kernels for 0% -> 0%
where the time goes in v1:
time: 516 us; the launch traced here: 510 us
  waiting for transfers between devices  264 us (51%)
  matrix products  89.8 us (17%)
  blocking collectives  40.7 us (8%)
  other arithmetic  38.9 us (8%)
  local copies, waits for them, and re-layouts  38.3 us (7%)
  starting transfers between devices  22.3 us (4%)
  between operations  15.9 us (3%)
    ppermute x25, waiting for transfers between devices, shift(): lax.ppermute(array, axis_name, [(i, (i + step) % size) for i in range(siz...  109 us
    reduce_scatter x1, waiting for transfers between devices, shards(): lax.psum_scatter(gate_up_weight_grad, 'fsdp', scatter_dimension=0, tiled=...  80.4 us
    all_gather x1, waiting for transfers between devices, shards(): down_full = lax.all_gather(down_pack, 'fsdp', axis=0, tiled=True)  42.4 us
    psum x1, blocking collectives, shards(): lax.psum(jnp.concatenate([operator_gain_grad, feedforward_gain_grad, quer...  40.7 us
    dot_general x8, matrix products, contract(): lax.dot_general(left, right, (((left_dim,), (right_dim,)), ((), ())), pre...  33.3 us
    all_gather x1, waiting for transfers between devices, shards(): attention_full = lax.all_gather(attention_pack, 'fsdp', axis=0, tiled=True)  31.1 us
    ppermute x25, starting transfers between devices, shift(): lax.ppermute(array, axis_name, [(i, (i + step) % size) for i in range(siz...  21.9 us
    unnamed x164, local copies, waits for them, and re-layouts  15.2 us
  transfers between devices with their start and end apart: 31, of which 19 were waited for; matrix products, arithmetic and copies ran while one was open for 26% of the time, Pallas kernels for 0%

profile of v1, /device:TPU:0, one launch (start us, length us, event | category | flops | bytes accessed | tf_op | source)
XLA Modules:
  0.0 509.7 jit_solution(16331534721619559554)
XLA Ops:
  18.8 9.8 %collective-permute-done = bf16[1,256,1024]{2,1,0:T(8,128)(2,1)S(1)} collective-permute-done((bf16[1,256,1024]{2,1,0:T(8,128)(2,1)S(1)}, bf16[1,256,1024]{2,1,0:T(8,128)(2,1)S(1)}, u32[]{:S(2)}, u32[]{:S(2)}) %collective-permute-start) | collective-permute-done | bytes 524320 | tf_op jit(solution)/shard_map/ppermute | solution.py:129
  31.9 31.1 %all-gather.4.cloned.1.call-done = bf16[1024,896]{0,1:T(8,128)(2,1)} async-done(((bf16[128,896]{0,1:T(8,128)(2,1)}), bf16[1024,896]{0,1:T(8,128)(2,1)}) %all-gather.4.cloned.1.call-update) | async-done | bytes 1835024 | tf_op jit(solution)/shard_map/all_gather | solution.py:244
  64.1 3.1 convolution_bitcast_fusion.3
  99.4 12.4 %collective-permute-done.3 = bf16[1,256,1024]{2,1,0:T(8,128)(2,1)S(1)} collective-permute-done((bf16[1,256,1024]{2,1,0:T(8,128)(2,1)S(1)}, bf16[1,256,1024]{2,1,0:T(8,128)(2,1)S(1)}, u32[]{:S(2)}, u32[]{:S(2)}) %collective-permute-start.3) | collective-permute-done | bytes 524320 | tf_op jit(solution)/shard_map/ppermute | solution.py:129
  113.9 11.7 %collective-permute-done.4 = bf16[1,256,1024]{2,1,0:T(8,128)(2,1)S(1)} collective-permute-done((bf16[1,256,1024]{2,1,0:T(8,128)(2,1)S(1)}, bf16[1,256,1024]{2,1,0:T(8,128)(2,1)S(1)}, u32[]{:S(2)}, u32[]{:S(2)}) %collective-permute-start.4) | collective-permute-done | bytes 524320 | tf_op jit(solution)/shard_map/ppermute | solution.py:129
  128.1 12.8 %collective-permute-done.9 = bf16[1,256,1024]{2,1,0:T(8,128)(2,1)S(1)} collective-permute-done((bf16[1,256,1024]{2,1,0:T(8,128)(2,1)S(1)}, bf16[1,256,1024]{2,1,0:T(8,128)(2,1)S(1)}, u32[]{:S(2)}, u32[]{:S(2)}) %collective-permute-start.9) | collective-permute-done | bytes 524320 | tf_op jit(solution)/shard_map/ppermute | solution.py:129
  143.3 11.5 %fusion.36 = f32[1024,2304]{1,0:T(8,128)} fusion(bf16[1024,2304]{1,0:T(8,128)(2,1)} %all-gather.6.cloned.1.call-done, bf16[1,512,1024]{2,1,0:T(8,128)(2,1)} %collective-permute-done.5, bf16[1,256,1024]{2,1,0:T(8,128)(2,1)} %copy-done.49, bf16[1,256,1024]{2,1,0:T(8,128)(2,1)S(1)} %multiply_convert_fusion.4), kind=kOutput, calls=%fused_computation.111 | convolution fusion | flops 4838129664 | bytes 16252928 | tf_op jit(solution)/shard_map/dot_general | solution.py:291
  154.9 42.4 %all-gather.8.cloned.1.call-done = bf16[1024,1152]{0,1:T(8,128)(2,1)} async-done(((bf16[128,1152]{0,1:T(8,128)(2,1)}), bf16[1024,1152]{0,1:T(8,128)(2,1)}) %all-gather.8.cloned.1.call-update) | async-done | bytes 2359312 | tf_op jit(solution)/shard_map/all_gather | solution.py:246
  197.3 9.1 %fusion.6 = (bf16[1024,1152]{1,0:T(8,128)(2,1)S(1)}, bf16[1024,1152]{1,0:T(8,128)(2,1)S(1)}, bf16[1024,1152]{1,0:T(8,128)(2,1)S(1)}) fusion(f32[1024,2304]{1,0:T(8,128)} %fusion.36, bf16[1024,1152]{0,1:T(8,128)(2,1)} %all-gather.8.cloned.1.call-done, bf16[1,512,1024]{2,1,0:T(8,128)(2,1)} %collective-permute-done.10, bf16[1,256,1024]{2,1,0:T(8,128)(2,1)} %copy-done.53, ...), kind=kOutput, calls=%fused_computation.18 | convolution fusion | flops 2441084928 | bytes 20971520 | tf_op jit(solution)/shard_map/dot_general | solution.py:294
  206.4 5.1 fusion.12
  216.3 12.5 %collective-permute-done.12 = bf16[1,256,1024]{2,1,0:T(8,128)(2,1)S(1)} collective-permute-done((bf16[1,256,1024]{2,1,0:T(8,128)(2,1)S(1)}, bf16[1,256,1024]{2,1,0:T(8,128)(2,1)S(1)}, u32[]{:S(2)}, u32[]{:S(2)}) %collective-permute-start.12) | collective-permute-done | bytes 524320 | tf_op jit(solution)/shard_map/ppermute | solution.py:129
  232.1 11.6 %collective-permute-done.13 = bf16[1,256,1024]{2,1,0:T(8,128)(2,1)S(1)} collective-permute-done((bf16[1,256,1024]{2,1,0:T(8,128)(2,1)S(1)}, bf16[1,256,1024]{2,1,0:T(8,128)(2,1)S(1)}, u32[]{:S(2)}, u32[]{:S(2)}) %collective-permute-start.13) | collective-permute-done | bytes 524320 | tf_op jit(solution)/shard_map/ppermute | solution.py:129
  245.6 5.6 %convolution_convert_fusion.1 = bf16[1024,1152]{1,0:T(8,128)(2,1)} fusion(bf16[1024,1152]{1,0:T(8,128)(2,1)S(1)} %get-tuple-element.35, bf16[1,512,1024]{2,1,0:T(8,128)(2,1)} %collective-permute-done.10, bf16[1,256,1024]{2,1,0:T(8,128)(2,1)S(1)} %copy-done.54, bf16[1,256,1024]{2,1,0:T(8,128)(2,1)S(1)} %constant_dynamic-slice_fusion), kind=kOutput, calls=%fused_computation.27 | convolution fusion | flops 2423390208 | bytes 6815744 | tf_op jit(solution)/shard_map/dot_general | solution.py:49
  254.2 5.5 %multiply_convert_fusion.1 = bf16[4,512,1024]{2,1,0:T(8,128)(2,1)S(1)} fusion(f32[4,512,1024]{2,1,0:T(8,128)} %copy-done.2, f32[4,512]{1,0:T(4,128)S(1)} %bitcast.212, f32[4,512]{1,0:T(4,128)S(1)} %log_add_fusion.1, pred[512,1024]{1,0:T(8,128)(4,1)S(1)} %copy-done.14, bf16[1024,4,64]{0,2,1:T(8,128)(2,1)S(1)} %bitcast.186, ...), kind=kOutput, calls=%fused_computation.1 | convolution fusion | flops 281018368 | bytes 13910016 | tf_op jit(solution)/shard_map/vmap(qhd,khd->hqk)/dot_general | solution.py:99
  259.8 3.5 multiply_convert_fusion
  270.7 3.8 fusion.22
  290.6 10.1 %convolution_convert_fusion = bf16[1024,2304]{1,0:T(8,128)(2,1)} fusion(bf16[1024,1152]{1,0:T(8,128)(2,1)} %copy-done.66, bf16[1024,1152]{1,0:T(8,128)(2,1)} %copy-done.65, bf16[1,512,1024]{2,1,0:T(8,128)(2,1)} %collective-permute-done.5, bf16[1,256,1024]{2,1,0:T(8,128)(2,1)S(1)} %copy-done.50, bf16[1,256,1024]{2,1,0:T(8,128)(2,1)S(1)} %copy-done.31), kind=kOutput, calls=%fused_computation.11 | convolution fusion | flops 4849926144 | bytes 11534336 | tf_op jit(solution)/shard_map/dot_general | solution.py:49
  300.7 5.4 %convolution_bitcast_fusion.2 = f32[1,1024,1024]{2,1,0:T(8,128)S(1)} fusion(bf16[1024,1152]{1,0:T(8,128)(2,1)} %copy-done.67, bf16[1024,1152]{0,1:T(8,128)(2,1)} %all-gather.8.cloned.1.call-done), kind=kOutput, calls=%fused_computation.32 | convolution fusion | flops 2415919104 | bytes 8912896 | tf_op jit(solution)/shard_map/dot_general | solution.py:49
  318.7 12.0 %collective-permute-done.7 = bf16[1,256,1024]{2,1,0:T(8,128)(2,1)S(1)} collective-permute-done((bf16[1,256,1024]{2,1,0:T(8,128)(2,1)S(1)}, bf16[1,256,1024]{2,1,0:T(8,128)(2,1)S(1)}, u32[]{:S(2)}, u32[]{:S(2)}) %collective-permute-start.7) | collective-permute-done | bytes 524320 | tf_op jit(solution)/shard_map/ppermute | solution.py:129
  332.0 9.5 %collective-permute-done.16 = bf16[1,256,1024]{2,1,0:T(8,128)(2,1)S(1)} collective-permute-done((bf16[1,256,1024]{2,1,0:T(8,128)(2,1)S(1)}, bf16[1,256,1024]{2,1,0:T(8,128)(2,1)S(1)}, u32[]{:S(2)}, u32[]{:S(2)}) %collective-permute-start.16) | collective-permute-done | bytes 524320 | tf_op jit(solution)/shard_map/ppermute | solution.py:129
  348.2 40.7 %psum.7 = f32[2176]{0:T(1024)S(1)} all-reduce(f32[2176]{0:T(1024)S(1)} %concatenate.102), channel_id=1, replica_groups=mesh['fsdp'=8,'ctx'=2,'tensor'=2] {'fsdp','ctx','tensor'}, use_global_device_ids=true, to_apply=%region_21.22 | all-reduce | flops 2176 | bytes 17408 | tf_op jit(solution)/shard_map/psum | solution.py:342
  405.0 80.4 %reduce-scatter.6.cloned.1.call-done = bf16[128,2304]{1,0:T(8,128)(2,1)} async-done(((bf16[1024,2304]{1,0:T(8,128)(2,1)}), bf16[128,2304]{1,0:T(8,128)(2,1)}) %reduce-scatter.6.cloned.1.call-update) | async-done | bytes 589840 | tf_op jit(solution)/shard_map/reduce_scatter | solution.py:302
  489.7 6.8 %collective-permute-done.23 = bf16[128,1152]{1,0:T(8,128)(2,1)S(1)} collective-permute-done((bf16[128,1152]{1,0:T(8,128)(2,1)S(1)}, bf16[128,1152]{1,0:T(8,128)(2,1)S(1)}, u32[]{:S(2)}, u32[]{:S(2)}) %collective-permute-start.23) | collective-permute-done | bytes 294944 | tf_op jit(solution)/shard_map/ppermute | solution.py:129
  497.7 3.8 collective-permute-done.22
  (356 shorter events, 133.5 us)
Async XLA Ops:
  7.2 55.8 %all-gather.4.cloned.1.call-start = ((), (), s32[]{:S(2)}) async-start(), calls=%async_computation.3 | async-start | bytes 2064384 | tf_op jit(solution)/shard_map/all_gather | solution.py:244
  12.5 130.9 %all-gather.6.cloned.1.call-start = ((), (), s32[]{:S(2)}) async-start(), calls=%async_computation.4 | async-start | bytes 5308416 | tf_op jit(solution)/shard_map/all_gather | solution.py:245
  13.8 14.9 %collective-permute-start = (bf16[1,256,1024]{2,1,0:T(8,128)(2,1)S(1)}, bf16[1,256,1024]{2,1,0:T(8,128)(2,1)S(1)}, u32[]{:S(2)}, u32[]{:S(2)}) collective-permute-start(bf16[1,256,1024]{2,1,0:T(8,128)(2,1)S(1)} %get-tuple-element.28), channel_id=1, source_target_pairs={{0,2},{2,0},{1,3},{3,1},{4,6},{6,4},{5,7},{7,5},{8,10},{10,8},{9,1... | collective-permute-start | bytes 1572872 | tf_op jit(solution)/shard_map/ppermute | solution.py:129
  18.7 178.6 %all-gather.8.cloned.1.call-start = ((), (), s32[]{:S(2)}) async-start(), calls=%async_computation.5 | async-start | bytes 2654208 | tf_op jit(solution)/shard_map/all_gather | solution.py:246
  93.7 251.7 %reduce-scatter.8.cloned.1.call-start = ((), (), s32[]{:S(2)}) async-start(), calls=%async_computation.7 | async-start | bytes 2654208 | tf_op jit(solution)/shard_map/reduce_scatter | solution.py:300
  97.8 14.0 %collective-permute-start.3 = (bf16[1,256,1024]{2,1,0:T(8,128)(2,1)S(1)}, bf16[1,256,1024]{2,1,0:T(8,128)(2,1)S(1)}, u32[]{:S(2)}, u32[]{:S(2)}) collective-permute-start(bf16[1,256,1024]{2,1,0:T(8,128)(2,1)S(1)} %slice.359), channel_id=1, source_target_pairs={{0,2},{2,0},{1,3},{3,1},{4,6},{6,4},{5,7},{7,5},{8,10},{10,8},{9,1... | collective-permute-start | bytes 1572872 | tf_op jit(solution)/shard_map/ppermute | solution.py:129
  112.3 13.3 %collective-permute-start.4 = (bf16[1,256,1024]{2,1,0:T(8,128)(2,1)S(1)}, bf16[1,256,1024]{2,1,0:T(8,128)(2,1)S(1)}, u32[]{:S(2)}, u32[]{:S(2)}) collective-permute-start(bf16[1,256,1024]{2,1,0:T(8,128)(2,1)S(1)} %multiply_convert_fusion.4), channel_id=1, source_target_pairs={{0,2},{2,0},{1,3},{3,1},{4,6},{6,4},{5,7},{7,5},{8,10},{10,8},{9,1... | collective-permute-start | bytes 1572872 | tf_op jit(solution)/shard_map/ppermute | solution.py:129
  126.4 16.3 %collective-permute-start.5 = (bf16[1,512,1024]{2,1,0:T(8,128)(2,1)S(1)}, bf16[1,512,1024]{2,1,0:T(8,128)(2,1)}, u32[]{:S(2)}, u32[]{:S(2)}) collective-permute-start(bf16[1,512,1024]{2,1,0:T(8,128)(2,1)S(1)} %pad_maximum_fusion.7), channel_id=1, source_target_pairs={{0,1},{1,0},{2,3},{3,2},{4,5},{5,4},{6,7},{7,6},{8,9},{9,8},{10,11... | collective-permute-start | bytes 3145736 | tf_op jit(solution)/shard_map/ppermute | solution.py:129
  126.5 14.4 %collective-permute-start.9 = (bf16[1,256,1024]{2,1,0:T(8,128)(2,1)S(1)}, bf16[1,256,1024]{2,1,0:T(8,128)(2,1)S(1)}, u32[]{:S(2)}, u32[]{:S(2)}) collective-permute-start(bf16[1,256,1024]{2,1,0:T(8,128)(2,1)S(1)} %constant_dynamic-slice_fusion), channel_id=1, source_target_pairs={{0,2},{2,0},{1,3},{3,1},{4,6},{6,4},{5,7},{7,5},{8,10},{10,8},{9,1... | collective-permute-start | bytes 1572872 | tf_op jit(solution)/shard_map/ppermute | solution.py:129
  142.7 12.2 %collective-permute-start.10 = (bf16[1,512,1024]{2,1,0:T(8,128)(2,1)}, bf16[1,512,1024]{2,1,0:T(8,128)(2,1)}, u32[]{:S(2)}, u32[]{:S(2)}) collective-permute-start(bf16[1,512,1024]{2,1,0:T(8,128)(2,1)} %pad_maximum_fusion.8), channel_id=1, source_target_pairs={{0,1},{1,0},{2,3},{3,2},{4,5},{5,4},{6,7},{7,6},{8,9},{9,8},{10,11... | collective-permute-start | bytes 3145736 | tf_op jit(solution)/shard_map/ppermute | solution.py:129
  214.8 14.0 %collective-permute-start.12 = (bf16[1,256,1024]{2,1,0:T(8,128)(2,1)S(1)}, bf16[1,256,1024]{2,1,0:T(8,128)(2,1)S(1)}, u32[]{:S(2)}, u32[]{:S(2)}) collective-permute-start(bf16[1,256,1024]{2,1,0:T(8,128)(2,1)S(1)} %slice.357), channel_id=1, source_target_pairs={{0,2},{2,0},{1,3},{3,1},{4,6},{6,4},{5,7},{7,5},{8,10},{10,8},{9,1... | collective-permute-start | bytes 1572872 | tf_op jit(solution)/shard_map/ppermute | solution.py:129
  230.6 13.1 %collective-permute-start.13 = (bf16[1,256,1024]{2,1,0:T(8,128)(2,1)S(1)}, bf16[1,256,1024]{2,1,0:T(8,128)(2,1)S(1)}, u32[]{:S(2)}, u32[]{:S(2)}) collective-permute-start(bf16[1,256,1024]{2,1,0:T(8,128)(2,1)S(1)} %get-tuple-element.25), channel_id=1, source_target_pairs={{0,2},{2,0},{1,3},{3,1},{4,6},{6,4},{5,7},{7,5},{8,10},{10,8},{9,1... | collective-permute-start | bytes 1572872 | tf_op jit(solution)/shard_map/ppermute | solution.py:129
  245.6 5.8 %collective-permute-start.14 = (bf16[1,512,1024]{2,1,0:T(8,128)(2,1)}, bf16[1,512,1024]{2,1,0:T(8,128)(2,1)}, u32[]{:S(2)}, u32[]{:S(2)}) collective-permute-start(bf16[1,512,1024]{2,1,0:T(8,128)(2,1)} %pad_maximum_fusion.9), channel_id=1, source_target_pairs={{0,1},{1,0},{2,3},{3,2},{4,5},{5,4},{6,7},{7,6},{8,9},{9,8},{10,11... | collective-permute-start | bytes 3145736 | tf_op jit(solution)/shard_map/ppermute | solution.py:129
  251.3 141.6 %reduce-scatter.10.cloned.1.call-start = ((), (), s32[]{:S(2)}) async-start(), calls=%async_computation.8 | async-start | bytes 1769472
  290.3 195.1 %reduce-scatter.6.cloned.1.call-start = ((), (), s32[]{:S(2)}) async-start(), calls=%async_computation.6 | async-start | bytes 5308416 | tf_op jit(solution)/shard_map/reduce_scatter | solution.py:302
  308.4 5.0 collective-permute-start.6
  315.9 14.9 %collective-permute-start.7 = (bf16[1,256,1024]{2,1,0:T(8,128)(2,1)S(1)}, bf16[1,256,1024]{2,1,0:T(8,128)(2,1)S(1)}, u32[]{:S(2)}, u32[]{:S(2)}) collective-permute-start(bf16[1,256,1024]{2,1,0:T(8,128)(2,1)S(1)} %slice.358), channel_id=1, source_target_pairs={{0,2},{2,0},{1,3},{3,1},{4,6},{6,4},{5,7},{7,5},{8,10},{10,8},{9,1... | collective-permute-start | bytes 1572872 | tf_op jit(solution)/shard_map/ppermute | solution.py:129
  318.0 23.5 %collective-permute-start.16 = (bf16[1,256,1024]{2,1,0:T(8,128)(2,1)S(1)}, bf16[1,256,1024]{2,1,0:T(8,128)(2,1)S(1)}, u32[]{:S(2)}, u32[]{:S(2)}) collective-permute-start(bf16[1,256,1024]{2,1,0:T(8,128)(2,1)S(1)} %slice.356), channel_id=1, source_target_pairs={{0,2},{2,0},{1,3},{3,1},{4,6},{6,4},{5,7},{7,5},{8,10},{10,8},{9,1... | collective-permute-start | bytes 1572872 | tf_op jit(solution)/shard_map/ppermute | solution.py:129
  331.9 11.6 %collective-permute-start.8 = (bf16[1,256,1024]{2,1,0:T(8,128)(2,1)}, bf16[1,256,1024]{2,1,0:T(8,128)(2,1)}, u32[]{:S(2)}, u32[]{:S(2)}) collective-permute-start(bf16[1,256,1024]{2,1,0:T(8,128)(2,1)} %get-tuple-element.30), channel_id=1, source_target_pairs={{0,1},{1,0},{2,3},{3,2},{4,5},{5,4},{6,7},{7,6},{8,9},{9,8},{10,11... | collective-permute-start | bytes 1572872 | tf_op jit(solution)/shard_map/ppermute | solution.py:129
  343.5 48.0 %collective-permute-start.17 = (f32[1,256,1024]{2,1,0:T(8,128)}, f32[1,256,1024]{2,1,0:T(8,128)}, u32[]{:S(2)}, u32[]{:S(2)}) collective-permute-start(f32[1,256,1024]{2,1,0:T(8,128)} %get-tuple-element.24), channel_id=1, source_target_pairs={{0,1},{1,0},{2,3},{3,2},{4,5},{5,4},{6,7},{7,6},{8,9},{9,8},{10,11... | collective-permute-start | bytes 3145736 | tf_op jit(solution)/shard_map/ppermute | solution.py:129
  346.6 43.6 %collective-permute-start.24 = (bf16[1152,128]{0,1:T(8,128)(2,1)}, bf16[1152,128]{0,1:T(8,128)(2,1)S(1)}, u32[]{:S(2)}, u32[]{:S(2)}) collective-permute-start(bf16[1152,128]{0,1:T(8,128)(2,1)} %bitcast.196), channel_id=1, source_target_pairs={{0,2},{2,0},{1,3},{3,1},{4,6},{6,4},{5,7},{7,5},{8,10},{10,8},{9,1... | collective-permute-start | bytes 884744 | tf_op jit(solution)/shard_map/ppermute | solution.py:129
  394.1 8.9 %collective-permute-start.21 = (bf16[256,128]{1,0:T(8,128)(2,1)S(1)}, bf16[256,128]{1,0:T(8,128)(2,1)S(1)}, u32[]{:S(2)}, u32[]{:S(2)}) collective-permute-start(bf16[256,128]{1,0:T(8,128)(2,1)S(1)} %bitcast.199), channel_id=1, source_target_pairs={{0,2},{2,0},{1,3},{3,1},{4,6},{6,4},{5,7},{7,5},{8,10},{10,8},{9,1... | collective-permute-start | bytes 196616 | tf_op jit(solution)/shard_map/ppermute | solution.py:129
  486.6 9.9 %collective-permute-start.23 = (bf16[128,1152]{1,0:T(8,128)(2,1)S(1)}, bf16[128,1152]{1,0:T(8,128)(2,1)S(1)}, u32[]{:S(2)}, u32[]{:S(2)}) collective-permute-start(bf16[128,1152]{1,0:T(8,128)(2,1)S(1)} %get-tuple-element.44), channel_id=1, source_target_pairs={{0,2},{2,0},{1,3},{3,1},{4,6},{6,4},{5,7},{7,5},{8,10},{10,8},{9,1... | collective-permute-start | bytes 884744 | tf_op jit(solution)/shard_map/ppermute | solution.py:129
  488.1 13.3 %collective-permute-start.22 = (bf16[128,1152]{1,0:T(8,128)(2,1)S(1)}, bf16[128,1152]{1,0:T(8,128)(2,1)S(1)}, u32[]{:S(2)}, u32[]{:S(2)}) collective-permute-start(bf16[128,1152]{1,0:T(8,128)(2,1)S(1)} %get-tuple-element.46), channel_id=1, source_target_pairs={{0,2},{2,0},{1,3},{3,1},{4,6},{6,4},{5,7},{7,5},{8,10},{10,8},{9,1... | collective-permute-start | bytes 884744 | tf_op jit(solution)/shard_map/ppermute | solution.py:129
  (81 other events, 918.0 us)
Sparse Core Ops, SparseCore 0:
  12.6 50.3 all-gather.3
  65.8 77.4 all-gather.5
  145.4 51.8 all-gather.7
  251.4 67.9 reduce-scatter.7
  322.6 64.6 reduce-scatter.9
  390.8 94.5 reduce-scatter.5
